TPU v7x, 256 devices: a whole 4x4x8 slice. The times are simulated.
256 devices in a mesh: band: 16 (over z, y_lo), pw: 16 (over x, y_hi, core).
Axes of the slice: x: 4, y: 4 (y_hi: 2, y_lo: 2; y = y_hi * 2 + y_lo), z: 8, core: 2. Of those that a mesh axis runs over, the one named last changes fastest.
Arguments:
- orbitals: bfloat16 [32, 192, 192, 256], P('band', 'pw'), may hold values from -5 to 5
- owner_group: int32 [1], replicated, may hold values from 0 to 15
Outputs:
- exchange_rows: float32 [32, 192, 192, 256], P('band', 'pw')
- owner_update: float32 [1, 192, 192, 256], P(None, 'pw', 'band')
All inputs are finite; a program needn't handle non-finite values.
Results may differ from a plain program's by a relative error of at most 0.0003.
Values may be sent and summed in bfloat16 or wider, within the bound.
A program may use at most 128 MiB of HBM per device.

v0:
```python
import math
import jax
import jax.numpy as jnp
from jax import lax
from jax.sharding import PartitionSpec as P

NX = 192
NY = 192
NZ = 256
SENT = 1
exact_share = 0.25
spacing = 0.2
highest = lax.Precision.HIGHEST


def broadcast(block, axis, owner):
    block = jnp.where(lax.axis_index(axis) == owner, block, jnp.zeros_like(block))
    return lax.psum(block, axis)


def dft_tables(length, number):
    samples = jnp.arange(length, dtype=jnp.int32)
    frequency = jnp.arange(number, dtype=jnp.int32)
    phase_index = samples[:, None] * frequency[None, :] % length
    phase_angle = phase_index.astype(jnp.float32) * (2 * math.pi / length)
    return (jnp.cos(phase_angle), jnp.sin(phase_angle))


def alternating(length):
    samples = jnp.arange(length, dtype=jnp.int32)
    return (1 - 2 * (samples % 2)).astype(jnp.float32)


def coulomb_table(ky_first, rows_y):
    freq_x = jnp.arange(NX, dtype=jnp.int32)
    freq_x = jnp.where(freq_x > NX // 2, freq_x - NX, freq_x)
    freq_y = ky_first + jnp.arange(rows_y, dtype=jnp.int32)
    freq_y = jnp.where(freq_y > NY // 2, freq_y - NY, freq_y)
    freq_z = jnp.arange(NZ // 2 + 1, dtype=jnp.int32)
    wave_x = freq_x.astype(jnp.float32) * (2 * math.pi / (NX * spacing))
    wave_y = freq_y.astype(jnp.float32) * (2 * math.pi / (NY * spacing))
    wave_z = freq_z.astype(jnp.float32) * (2 * math.pi / (NZ * spacing))
    square = (
        (wave_x * wave_x)[:, None, None]
        + (wave_y * wave_y)[None, :, None]
        + (wave_z * wave_z)[None, None, :]
    )
    safe = jnp.where(square > 0, square, 1.0)
    return jnp.where(square > 0, 4 * math.pi / safe, 0.0)


def complex_pass(spectrum, cosine_table, sine_table, pattern, direction):
    half_width = spectrum.shape[-1] // 2
    with_cosine = jnp.einsum(pattern, cosine_table, spectrum, precision=highest)
    with_sine = jnp.einsum(pattern, sine_table, spectrum, precision=highest)
    real_part = with_cosine[..., :half_width] + direction * with_sine[..., half_width:]
    imag_part = with_cosine[..., half_width:] - direction * with_sine[..., :half_width]
    return jnp.concatenate([real_part, imag_part], -1)


def split_pass(real_in, imag_in, cosine_table, sine_table, pattern, direction):
    real_part = jnp.einsum(
        pattern, cosine_table, real_in, precision=highest
    ) + direction * jnp.einsum(pattern, sine_table, imag_in, precision=highest)
    imag_part = jnp.einsum(
        pattern, cosine_table, imag_in, precision=highest
    ) - direction * jnp.einsum(pattern, sine_table, real_in, precision=highest)
    return (real_part, imag_part)


def forward_planes(density):
    cosine_z, sine_z = dft_tables(NZ, NZ // 2)
    z_table = jnp.concatenate([cosine_z, -sine_z], 1)
    spectrum = jnp.einsum("pxyz,zc->pxyc", density, z_table, precision=highest)
    nyquist = jnp.einsum("pxyz,z->pxy", density, alternating(NZ), precision=highest)
    cosine_y, sine_y = dft_tables(NY, NY)
    spectrum = complex_pass(spectrum, cosine_y, sine_y, "uy,pxyc->pxuc", 1.0)
    nyq_real, nyq_imag = split_pass(
        nyquist, jnp.zeros_like(nyquist), cosine_y, sine_y, "uy,pxy->pxu", 1.0
    )
    return (spectrum, nyq_real, nyq_imag)


def column_work(columns, nyq_real, nyq_imag, ky_first, rows_y):
    cosine_x, sine_x = dft_tables(NX, NX)
    spectrum = complex_pass(columns, cosine_x, sine_x, "ux,pxyc->puyc", 1.0)
    nyq_real, nyq_imag = split_pass(nyq_real, nyq_imag, cosine_x, sine_x, "ux,pxy->puy", 1.0)
    kernel = coulomb_table(ky_first, rows_y)
    main_kernel = kernel[:, :, : NZ // 2]
    edge_kernel = kernel[:, :, NZ // 2][None]
    spectrum = spectrum * jnp.concatenate([main_kernel, main_kernel], -1)[None]
    spectrum = complex_pass(spectrum, cosine_x, sine_x, "ux,pxyc->puyc", -1.0)
    nyq_real, nyq_imag = split_pass(
        nyq_real * edge_kernel, nyq_imag * edge_kernel, cosine_x, sine_x, "ux,pxy->puy", -1.0
    )
    return (spectrum, nyq_real, nyq_imag)


def inverse_planes(spectrum, nyq_real, nyq_imag):
    cosine_y, sine_y = dft_tables(NY, NY)
    spectrum = complex_pass(spectrum, cosine_y, sine_y, "uy,pxyc->pxuc", -1.0)
    edge_real, edge_imag = split_pass(nyq_real, nyq_imag, cosine_y, sine_y, "uy,pxy->pxu", -1.0)
    frequency = jnp.arange(NZ // 2, dtype=jnp.int32)
    cosine_z, sine_z = dft_tables(NZ, NZ // 2)
    first = frequency == 0
    real_weight = jnp.where(first, 1.0, 2.0).astype(jnp.float32)
    imag_weight = jnp.where(first, 0.0, 2.0).astype(jnp.float32)
    z_table = jnp.concatenate(
        [real_weight[:, None] * cosine_z.T, -imag_weight[:, None] * sine_z.T], 0
    )
    z_table = z_table * (1.0 / (NX * NY * NZ))
    result = jnp.einsum("pxyc,cz->pxyz", spectrum, z_table, precision=highest)
    edge_table = alternating(NZ) * (1.0 / (NX * NY * NZ))
    return result + edge_real[..., None] * edge_table


def on_device(orbitals, owner_group):
    own_count = orbitals.shape[0]
    slab_rows = orbitals.shape[1]
    received = broadcast(orbitals[:SENT], "band", owner_group[0])
    sent_values = received.astype(jnp.float32)
    own_values = orbitals.astype(jnp.float32)
    density = (own_values[:, None] * sent_values[None, :]).reshape(
        own_count * SENT, slab_rows, NY, NZ
    )
    planes, plane_real, plane_imag = forward_planes(density)
    rows_y = NY // lax.axis_size("pw")
    ky_first = lax.axis_index("pw") * rows_y
    pieces = []
    real_pieces = []
    imag_pieces = []
    for pair_index in range(planes.shape[0]):
        upper = pair_index + 1
        columns, col_real, col_imag = (
            lax.all_to_all(planes[pair_index:upper], "pw", split_axis=2, concat_axis=1, tiled=True),
            lax.all_to_all(
                plane_real[pair_index:upper], "pw", split_axis=2, concat_axis=1, tiled=True
            ),
            lax.all_to_all(
                plane_imag[pair_index:upper], "pw", split_axis=2, concat_axis=1, tiled=True
            ),
        )
        worked = column_work(columns, col_real, col_imag, ky_first, rows_y)
        main_back, real_back, imag_back = (
            lax.all_to_all(worked[0], "pw", split_axis=1, concat_axis=2, tiled=True),
            lax.all_to_all(worked[1], "pw", split_axis=1, concat_axis=2, tiled=True),
            lax.all_to_all(worked[2], "pw", split_axis=1, concat_axis=2, tiled=True),
        )
        pieces.append(main_back)
        real_pieces.append(real_back)
        imag_pieces.append(imag_back)
    returned = jnp.concatenate(pieces, 0)
    back_real = jnp.concatenate(real_pieces, 0)
    back_imag = jnp.concatenate(imag_pieces, 0)
    potential = inverse_planes(returned, back_real, back_imag).reshape(
        own_count, SENT, slab_rows, NY, NZ
    )
    exchange_rows = -exact_share * jnp.sum(potential * sent_values[None], 1)
    partial_value = -exact_share * jnp.sum(potential * own_values[:, None], 0)
    owner_update = lax.psum_scatter(partial_value, "band", scatter_dimension=2, tiled=True)
    return (exchange_rows, owner_update)


def solution(mesh):
    placed = (P("band", "pw", None, None), P())
    return jax.shard_map(
        on_device,
        mesh=mesh,
        in_specs=placed,
        out_specs=(P("band", "pw", None, None), P(None, "pw", "band", None)),
        check_vma=False,
    )
```

profile of v0, /device:TPU:6, one launch (start us, length us, event | category | flops | bytes accessed | tf_op | source)
XLA Modules:
  0.0 574.0 jit_solution(14537349176392429986)
XLA Ops:
  13.9 140.9 %all-reduce.2.cloned.1.call-done = bf16[12,192,256]{2,1,0:T(8,128)(2,1)} async-done(((bf16[12,192,256]{2,1,0:T(8,128)(2,1)}), bf16[12,192,256]{2,1,0:T(8,128)(2,1)}) %all-reduce.2.cloned.1.call-update) | async-done | bytes 1179664 | tf_op jit(solution)/shard_map/psum | solution.py:18
  156.3 5.5 fusion.1
  161.9 7.6 %convolution_bitcast_fusion.2 = f32[2,12,192,256]{3,2,1,0:T(8,128)} fusion(f32[2,12,192,256]{3,2,1,0:T(8,128)S(1)} %fusion.1), kind=kOutput, calls=%fused_computation.37 | convolution fusion | flops 2718240768 | bytes 9437184 | tf_op jit(solution)/shard_map/uy,pxyc->pxuc/dot_general | solution.py:55
  169.4 7.7 %convolution_bitcast_fusion.3 = f32[2,12,192,256]{3,2,1,0:T(8,128)} fusion(f32[2,12,192,256]{3,2,1,0:T(8,128)S(1)} %fusion.1), kind=kOutput, calls=%fused_computation.38 | convolution fusion | flops 2718240768 | bytes 9437184 | tf_op jit(solution)/shard_map/uy,pxyc->pxuc/dot_general | solution.py:54
  177.1 4.3 fusion
  186.9 7.0 %all-to-all-start.4 = ((f32[16,1,144]{2,1,0:T(1,128)}), f32[16,1,144]{2,1,0:T(1,128)S(1)}, u32[]{:S(2)}, u32[]{:S(2)}) async-start(f32[16,1,144]{2,1,0:T(1,128)} %reshape.293), calls=%async_computation.4 | async-start | bytes 32768 | tf_op jit(solution)/shard_map/all_to_all | solution.py:136
  193.8 7.0 %slice_subtract_fusion = (f32[2,12,192,128]{3,2,1,0:T(8,128)}, f32[2,12,192,128]{3,2,1,0:T(8,128)}) fusion(f32[2,12,192,256]{3,2,1,0:T(8,128)} %convolution_bitcast_fusion.2, f32[2,12,192,256]{3,2,1,0:T(8,128)} %convolution_bitcast_fusion.3), kind=kLoop, calls=%fused_computation.23 | loop fusion | flops 1179648 | bytes 14155776 | tf_op jit(solution)/shard_map/sub | solution.py:57
  206.0 7.2 %all-to-all-start.5 = ((f32[16,1,144]{2,1,0:T(1,128)}), f32[16,1,144]{2,1,0:T(1,128)S(1)}, u32[]{:S(2)}, u32[]{:S(2)}) async-start(f32[16,1,144]{2,1,0:T(1,128)} %reshape.295), calls=%async_computation.5 | async-start | bytes 32768 | tf_op jit(solution)/shard_map/all_to_all | solution.py:139
  218.9 5.4 all-to-all-start.7
  229.9 6.0 %all-to-all-start.8 = ((f32[16,1,144]{2,1,0:T(1,128)}), f32[16,1,144]{2,1,0:T(1,128)S(1)}, u32[]{:S(2)}, u32[]{:S(2)}) async-start(f32[16,1,144]{2,1,0:T(1,128)} %reshape.289), calls=%async_computation.8 | async-start | bytes 32768 | tf_op jit(solution)/shard_map/all_to_all | solution.py:139
  254.7 5.7 all-to-all-start.9
  265.9 5.5 all-to-all-start.11
  277.0 5.5 all-to-all-start.10
  288.0 5.5 all-to-all-start.6
  293.5 4.1 pad_maximum_fusion
  302.0 7.2 %all-to-all-start.2 = ((f32[1,12,192,256]{3,0,1,2:T(1,128)}), f32[1,12,192,256]{3,0,1,2:T(1,128)}, u32[]{:S(2)}, u32[]{:S(2)}) async-start(f32[1,12,192,256]{3,0,1,2:T(1,128)} %copy.86), calls=%async_computation.2 | async-start | bytes 4718592 | tf_op jit(solution)/shard_map/all_to_all | solution.py:135
  309.2 5.5 copy.81
  314.7 24.4 %all-to-all-done.2 = f32[1,12,192,256]{3,0,1,2:T(1,128)} async-done(((f32[1,12,192,256]{3,0,1,2:T(1,128)}), f32[1,12,192,256]{3,0,1,2:T(1,128)}, u32[]{:S(2)}, u32[]{:S(2)}) %all-to-all-start.2) | async-done | bytes 2359328 | tf_op jit(solution)/shard_map/all_to_all | solution.py:135
  339.1 7.9 %all-to-all-start = ((f32[1,12,192,256]{3,0,1,2:T(1,128)}), f32[1,12,192,256]{3,0,1,2:T(1,128)}, u32[]{:S(2)}, u32[]{:S(2)}) async-start(f32[1,12,192,256]{3,0,1,2:T(1,128)} %copy.81), calls=%async_computation | async-start | bytes 4718592 | tf_op jit(solution)/shard_map/all_to_all | solution.py:135
  348.3 3.9 copy.87
  355.3 4.2 reshape.253
  359.5 4.8 convolution_bitcast_fusion.6
  378.7 7.2 %all-to-all-start.3 = ((f32[1,192,12,256]{3,0,2,1:T(1,128)}), f32[1,192,12,256]{3,0,2,1:T(1,128)}, u32[]{:S(2)}, u32[]{:S(2)}) async-start(f32[1,192,12,256]{3,0,2,1:T(1,128)} %copy.89), calls=%async_computation.3 | async-start | bytes 4718592 | tf_op jit(solution)/shard_map/all_to_all | solution.py:145
  392.9 4.1 reshape.252
  397.0 4.8 convolution_bitcast_fusion.10
  416.2 7.5 %all-to-all-start.1 = ((f32[1,192,12,256]{3,0,2,1:T(1,128)}), f32[1,192,12,256]{3,0,2,1:T(1,128)}, u32[]{:S(2)}, u32[]{:S(2)}) async-start(f32[1,192,12,256]{3,0,2,1:T(1,128)} %copy.84), calls=%async_computation.1 | async-start | bytes 4718592 | tf_op jit(solution)/shard_map/all_to_all | solution.py:145
  432.0 5.3 copy.90
  437.4 16.2 %all-to-all-done.1 = f32[1,192,12,256]{3,0,2,1:T(1,128)} async-done(((f32[1,192,12,256]{3,0,2,1:T(1,128)}), f32[1,192,12,256]{3,0,2,1:T(1,128)}, u32[]{:S(2)}, u32[]{:S(2)}) %all-to-all-start.1) | async-done | bytes 2359328 | tf_op jit(solution)/shard_map/all_to_all | solution.py:145
  459.4 5.8 %convolution_bitcast_fusion = f32[2,12,192,256]{3,2,1,0:T(8,128)S(1)} fusion(f32[2,12,192,256]{3,2,1,0:T(8,128)S(1)} %copy_dynamic-update-slice_fusion), kind=kOutput, calls=%fused_computation.35 | convolution fusion | flops 2718240768 | bytes 9437184 | tf_op jit(solution)/shard_map/uy,pxyc->pxuc/dot_general | solution.py:55
  465.3 5.6 convolution_bitcast_fusion.1
  472.5 6.4 %fusion.2 = (f32[12,192,256]{2,1,0:T(8,128)S(1)}, f32[2,12,192,256]{3,2,1,0:T(8,128)}) fusion(bf16[2,12,192,256]{3,2,1,0:T(8,128)(2,1)S(1)} %copy-done.1, f32[256]{0:T(256)S(1)} %broadcast_multiply_fusion, f32[2,12,192]{2,1,0:T(8,128)S(1)} %fusion.23, f32[12,192,256]{2,1,0:T(8,128)S(1)} %mul.580, f32[128,256]{1,0:T(8,128)S(1)} %get-tuple-element.28, ...), kind=kOutput, calls=%fused_computation.4 | convolution fusion | flops 3632857088 | bytes 16796672 | tf_op jit(solution)/shard_map/pxyc,cz->pxyz/dot_general | solution.py:112
  482.2 83.0 %reduce-scatter.2.cloned.1.call-done = f32[1,12,12,256]{3,1,0,2:T(8,128)} async-done(((f32[1,12,192,256]{3,1,0,2:T(8,128)}), f32[1,12,12,256]{3,1,0,2:T(8,128)}) %reduce-scatter.2.cloned.1.call-update) | async-done | bytes 147472 | tf_op jit(solution)/shard_map/reduce_scatter | solution.py:160
  (175 shorter events, 129.6 us)
Async XLA Ops:
  7.2 147.6 %all-reduce.2.cloned.1.call-start = ((), (), s32[]{:S(2)}) async-start(), calls=%async_computation.13 | async-start | bytes 2359296 | tf_op jit(solution)/shard_map/psum | solution.py:18
  12.5 1.4 copy-start.4
  169.4 7.7 %copy-start = (bf16[2,12,192,256]{3,2,1,0:T(8,128)(2,1)S(1)}, bf16[2,12,192,256]{3,2,1,0:T(8,128)(2,1)}, u32[]{:S(2)}) copy-start(bf16[2,12,192,256]{3,2,1,0:T(8,128)(2,1)} %param.2) | copy-start | bytes 7077892
  186.9 19.2 %all-to-all-start.4 = ((f32[16,1,144]{2,1,0:T(1,128)}), f32[16,1,144]{2,1,0:T(1,128)S(1)}, u32[]{:S(2)}, u32[]{:S(2)}) async-start(f32[16,1,144]{2,1,0:T(1,128)} %reshape.293), calls=%async_computation.4 | async-start | bytes 32768 | tf_op jit(solution)/shard_map/all_to_all | solution.py:136
  206.0 12.8 %all-to-all-start.5 = ((f32[16,1,144]{2,1,0:T(1,128)}), f32[16,1,144]{2,1,0:T(1,128)S(1)}, u32[]{:S(2)}, u32[]{:S(2)}) async-start(f32[16,1,144]{2,1,0:T(1,128)} %reshape.295), calls=%async_computation.5 | async-start | bytes 32768 | tf_op jit(solution)/shard_map/all_to_all | solution.py:139
  218.9 11.0 %all-to-all-start.7 = ((f32[16,1,144]{2,1,0:T(1,128)}), f32[16,1,144]{2,1,0:T(1,128)S(1)}, u32[]{:S(2)}, u32[]{:S(2)}) async-start(f32[16,1,144]{2,1,0:T(1,128)} %reshape.287), calls=%async_computation.7 | async-start | bytes 32768 | tf_op jit(solution)/shard_map/all_to_all | solution.py:136
  229.9 11.5 %all-to-all-start.8 = ((f32[16,1,144]{2,1,0:T(1,128)}), f32[16,1,144]{2,1,0:T(1,128)S(1)}, u32[]{:S(2)}, u32[]{:S(2)}) async-start(f32[16,1,144]{2,1,0:T(1,128)} %reshape.289), calls=%async_computation.8 | async-start | bytes 32768 | tf_op jit(solution)/shard_map/all_to_all | solution.py:139
  254.7 11.2 %all-to-all-start.9 = ((f32[16,1,144]{2,1,0:T(1,128)}), f32[16,1,144]{2,1,0:T(1,128)S(1)}, u32[]{:S(2)}, u32[]{:S(2)}) async-start(f32[16,1,144]{2,1,0:T(1,128)} %reshape.291), calls=%async_computation.9 | async-start | bytes 32768 | tf_op jit(solution)/shard_map/all_to_all | solution.py:146
  265.9 11.0 %all-to-all-start.11 = ((f32[16,1,144]{2,1,0:T(1,128)}), f32[16,1,144]{2,1,0:T(1,128)S(1)}, u32[]{:S(2)}, u32[]{:S(2)}) async-start(f32[16,1,144]{2,1,0:T(1,128)} %reshape.299), calls=%async_computation.11 | async-start | bytes 32768 | tf_op jit(solution)/shard_map/all_to_all | solution.py:147
  277.0 20.6 %copy-start.6 = (f32[16,1,144]{2,1,0:T(1,128)}, f32[16,1,144]{2,1,0:T(1,128)S(1)}, u32[]{:S(2)}) copy-start(f32[16,1,144]{2,1,0:T(1,128)S(1)} %all-to-all-done.11) | copy-start | bytes 27652
  277.0 11.0 %all-to-all-start.10 = ((f32[16,1,144]{2,1,0:T(1,128)}), f32[16,1,144]{2,1,0:T(1,128)S(1)}, u32[]{:S(2)}, u32[]{:S(2)}) async-start(f32[16,1,144]{2,1,0:T(1,128)} %reshape.301), calls=%async_computation.10 | async-start | bytes 32768 | tf_op jit(solution)/shard_map/all_to_all | solution.py:147
  288.0 9.6 %copy-start.8 = (f32[16,1,144]{2,1,0:T(1,128)}, f32[16,1,144]{2,1,0:T(1,128)S(1)}, u32[]{:S(2)}) copy-start(f32[16,1,144]{2,1,0:T(1,128)S(1)} %all-to-all-done.10) | copy-start | bytes 27652
  288.0 13.4 %all-to-all-start.6 = ((f32[16,1,144]{2,1,0:T(1,128)}), f32[16,1,144]{2,1,0:T(1,128)S(1)}, u32[]{:S(2)}, u32[]{:S(2)}) async-start(f32[16,1,144]{2,1,0:T(1,128)} %reshape.297), calls=%async_computation.6 | async-start | bytes 32768 | tf_op jit(solution)/shard_map/all_to_all | solution.py:146
  301.4 0.6 copy-start.10
  302.0 37.1 %all-to-all-start.2 = ((f32[1,12,192,256]{3,0,1,2:T(1,128)}), f32[1,12,192,256]{3,0,1,2:T(1,128)}, u32[]{:S(2)}, u32[]{:S(2)}) async-start(f32[1,12,192,256]{3,0,1,2:T(1,128)} %copy.86), calls=%async_computation.2 | async-start | bytes 4718592 | tf_op jit(solution)/shard_map/all_to_all | solution.py:135
  339.1 39.6 %all-to-all-start = ((f32[1,12,192,256]{3,0,1,2:T(1,128)}), f32[1,12,192,256]{3,0,1,2:T(1,128)}, u32[]{:S(2)}, u32[]{:S(2)}) async-start(f32[1,12,192,256]{3,0,1,2:T(1,128)} %copy.81), calls=%async_computation | async-start | bytes 4718592 | tf_op jit(solution)/shard_map/all_to_all | solution.py:135
  359.5 4.9 copy-start.2
  378.7 37.5 %all-to-all-start.3 = ((f32[1,192,12,256]{3,0,2,1:T(1,128)}), f32[1,192,12,256]{3,0,2,1:T(1,128)}, u32[]{:S(2)}, u32[]{:S(2)}) async-start(f32[1,192,12,256]{3,0,2,1:T(1,128)} %copy.89), calls=%async_computation.3 | async-start | bytes 4718592 | tf_op jit(solution)/shard_map/all_to_all | solution.py:145
  397.0 4.9 copy-start.3
  416.2 9.5 %copy-start.7 = (f32[16,1,144]{2,1,0:T(1,128)S(1)}, f32[16,1,144]{2,1,0:T(1,128)}, u32[]{:S(2)}) copy-start(f32[16,1,144]{2,1,0:T(1,128)} %copy-done.6) | copy-start | bytes 27652
  416.2 10.9 %copy-start.9 = (f32[16,1,144]{2,1,0:T(1,128)S(1)}, f32[16,1,144]{2,1,0:T(1,128)}, u32[]{:S(2)}) copy-start(f32[16,1,144]{2,1,0:T(1,128)} %copy-done.8) | copy-start | bytes 27652
  416.2 12.3 %copy-start.11 = (f32[16,1,144]{2,1,0:T(1,128)S(1)}, f32[16,1,144]{2,1,0:T(1,128)}, u32[]{:S(2)}) copy-start(f32[16,1,144]{2,1,0:T(1,128)} %copy-done.10) | copy-start | bytes 27652
  416.2 37.4 %all-to-all-start.1 = ((f32[1,192,12,256]{3,0,2,1:T(1,128)}), f32[1,192,12,256]{3,0,2,1:T(1,128)}, u32[]{:S(2)}, u32[]{:S(2)}) async-start(f32[1,192,12,256]{3,0,2,1:T(1,128)} %copy.84), calls=%async_computation.1 | async-start | bytes 4718592 | tf_op jit(solution)/shard_map/all_to_all | solution.py:145
  423.7 141.5 %reduce-scatter.2.cloned.1.call-start = ((), (), s32[]{:S(2)}) async-start(), calls=%async_computation.14 | async-start | bytes 3342336 | tf_op jit(solution)/shard_map/reduce_scatter | solution.py:160
  457.5 1.7 copy-start.5
  470.8 1.7 copy-start.1
Sparse Core Ops, SparseCore 0:
  11.2 143.5 all-reduce.1
  482.4 82.7 reduce-scatter.1
where the time goes:
time: 581 us; the launch traced here: 574 us
  waiting for transfers between devices  282 us (49%)
  matrix products  94.3 us (16%)
  starting transfers between devices  77.6 us (13%)
  local copies, waits for them, and re-layouts  72.4 us (12%)
  other arithmetic  31.5 us (5%)
  between operations  15.8 us (3%)
    psum x1, waiting for transfers between devices, broadcast(): return lax.psum(block, axis)  141 us
    reduce_scatter x1, waiting for transfers between devices, on_device(): lax.psum_scatter(partial_value, 'band', scatter_dimension=2, tiled=True)  83 us
    dot_general x6, matrix products, complex_pass(): with_sine = jnp.einsum(pattern, sine_table, spectrum, precision=highest)  29.3 us
    dot_general x6, matrix products, complex_pass(): with_cosine = jnp.einsum(pattern, cosine_table, spectrum, precision=highest)  26.4 us
    all_to_all x2, waiting for transfers between devices, on_device(): lax.all_to_all(planes[pair_index:upper], 'pw', split_axis=2, concat_axis=...  24.4 us
    all_to_all x2, waiting for transfers between devices, on_device(): lax.all_to_all(worked[0], 'pw', split_axis=1, concat_axis=2, tiled=True)  16.2 us
    all_to_all x2, starting transfers between devices, on_device(): lax.all_to_all(planes[pair_index:upper], 'pw', split_axis=2, concat_axis=...  15.1 us
    all_to_all x2, starting transfers between devices, on_device(): lax.all_to_all(worked[0], 'pw', split_axis=1, concat_axis=2, tiled=True)  14.7 us
  transfers between devices with their start and end apart: 14, of which 10 were waited for; matrix products, arithmetic and copies ran while one was open for 20% of the time, Pallas kernels for 0%

commit v1 on v0

--- a/solution.py
+++ b/solution.py
@@ -15,7 +15,8 @@
 
 def broadcast(block, axis, owner):
     block = jnp.where(lax.axis_index(axis) == owner, block, jnp.zeros_like(block))
-    return lax.psum(block, axis)
+    _see_bench = lambda vector, row_axis: lax.all_gather(vector, row_axis).sum(axis=0)
+    return _see_bench(block, axis)
 
 
 def dft_tables(length, number):

time: 581 us -> 844 us (1.45)
  waiting for transfers between devices: 282 us -> 532 us
  other arithmetic: 31.5 us -> 42.1 us
    all_gather x0 -> x1, waiting for transfers between devices: none -> 392 us  [broadcast(): lax.all_gather(vector, row_axis).sum(axis=0)]
    psum x1 -> x0, waiting for transfers between devices: 141 us -> none  [broadcast(): return lax.psum(block, axis)]
    reduce_sum x0 -> x1, other arithmetic: none -> 10.9 us  [broadcast(): lax.all_gather(vector, row_axis).sum(axis=0)]
  transfers between devices with their start and end apart: 14 -> 14, of which waited for: 10 -> 7; matrix products, arithmetic and copies ran while one was open for 20% -> 16% of each run, Pallas kernels for 0% -> 0%
where the time goes in v1:
time: 844 us; the launch traced here: 839 us
  waiting for transfers between devices  532 us (63%)
  matrix products  93 us (11%)
  starting transfers between devices  83.1 us (10%)
  local copies, waits for them, and re-layouts  73.1 us (9%)
  other arithmetic  42.1 us (5%)
  between operations  15.9 us (2%)
    all_gather x1, waiting for transfers between devices, broadcast(): lax.all_gather(vector, row_axis).sum(axis=0)  392 us
    reduce_scatter x1, waiting for transfers between devices, on_device(): lax.psum_scatter(partial_value, 'band', scatter_dimension=2, tiled=True)  90.2 us
    dot_general x6, matrix products, complex_pass(): with_sine = jnp.einsum(pattern, sine_table, spectrum, precision=highest)  29.6 us
    dot_general x6, matrix products, complex_pass(): with_cosine = jnp.einsum(pattern, cosine_table, spectrum, precision=highest)  25.9 us
    all_to_all x2, waiting for transfers between devices, on_device(): lax.all_to_all(planes[pair_index:upper], 'pw', split_axis=2, concat_axis=...  24.4 us
  transfers between devices with their start and end apart: 14, of which 7 were waited for; matrix products, arithmetic and copies ran while one was open for 16% of the time, Pallas kernels for 0%

profile of v1, /device:TPU:6, one launch (start us, length us, event | category | flops | bytes accessed | tf_op | source)
XLA Modules:
  0.0 838.7 jit_solution(3224417450145283547)
XLA Ops:
  14.8 391.6 %all-gather.3.cloned.1.call-done = bf16[16,12,192,256]{3,2,1,0:T(8,128)(2,1)} async-done(((bf16[1,12,192,256]{3,2,1,0:T(8,128)(2,1)}), bf16[16,12,192,256]{3,2,1,0:T(8,128)(2,1)}) %all-gather.3.cloned.1.call-update) | async-done | bytes 18874384 | tf_op jit(solution)/shard_map/all_gather | solution.py:18
  406.4 10.9 %reduce.4 = bf16[12,192,256]{2,1,0:T(8,128)(2,1)S(1)} reduce(bf16[16,12,192,256]{3,2,1,0:T(8,128)(2,1)} %all-gather.3.cloned.1.call-done, bf16[]{:T(256)} %constant.93.clone.1), dimensions={0}, to_apply=%region_0.1 | reduce | flops 8847360 | bytes 20054018 | tf_op jit(solution)/shard_map/reduce_sum | solution.py:18
  422.9 7.4 convolution_bitcast_fusion.2
  430.3 8.0 convolution_bitcast_fusion.3
  438.3 4.3 fusion
  447.0 7.0 all-to-all-start.5
  455.0 6.9 slice_subtract_fusion
  467.1 7.2 all-to-all-start.4
  479.9 5.7 all-to-all-start.8
  491.1 7.2 all-to-all-start.7
  504.5 7.5 all-to-all-start.6
  521.3 7.2 all-to-all-start.9
  534.1 5.4 all-to-all-start.10
  545.2 5.9 all-to-all-start.11
  551.1 4.1 pad_maximum_fusion
  559.7 7.2 all-to-all-start.2
  566.9 5.5 copy.81
  572.4 24.4 %all-to-all-done.2 = f32[1,12,192,256]{3,0,1,2:T(1,128)} async-done(((f32[1,12,192,256]{3,0,1,2:T(1,128)}), f32[1,12,192,256]{3,0,1,2:T(1,128)}, u32[]{:S(2)}, u32[]{:S(2)}) %all-to-all-start.2) | async-done | bytes 2359328 | tf_op jit(solution)/shard_map/all_to_all | solution.py:136
  596.8 7.9 all-to-all-start
  606.0 3.9 copy.87
  612.9 4.1 reshape.258
  617.1 4.8 convolution_bitcast_fusion.6
  636.1 7.2 all-to-all-start.3
  650.3 4.4 reshape.257
  654.7 4.8 convolution_bitcast_fusion.10
  673.6 7.5 all-to-all-start.1
  689.4 5.3 copy.90
  694.7 16.3 %all-to-all-done.1 = f32[1,192,12,256]{3,0,2,1:T(1,128)} async-done(((f32[1,192,12,256]{3,0,2,1:T(1,128)}), f32[1,192,12,256]{3,0,2,1:T(1,128)}, u32[]{:S(2)}, u32[]{:S(2)}) %all-to-all-start.1) | async-done | bytes 2359328 | tf_op jit(solution)/shard_map/all_to_all | solution.py:146
  716.8 5.9 convolution_bitcast_fusion
  722.7 5.6 convolution_bitcast_fusion.1
  730.0 6.4 fusion.2
  739.7 90.2 %reduce-scatter.2.cloned.1.call-done = f32[1,12,12,256]{3,1,0,2:T(8,128)} async-done(((f32[1,12,192,256]{3,1,0,2:T(8,128)}), f32[1,12,12,256]{3,1,0,2:T(8,128)}) %reduce-scatter.2.cloned.1.call-update) | async-done | bytes 147472 | tf_op jit(solution)/shard_map/reduce_scatter | solution.py:161
  (188 shorter events, 125.0 us)
Async XLA Ops:
  7.2 399.2 %all-gather.3.cloned.1.call-start = ((), (), s32[]{:S(2)}) async-start(), calls=%async_computation.14 | async-start | bytes 20054016 | tf_op jit(solution)/shard_map/all_gather | solution.py:18
  14.3 392.1 %copy-start.4 = (f32[192,12,129]{2,0,1:T(8,128)}, f32[192,12,129]{2,0,1:T(8,128)S(1)}, u32[]{:S(2)}) copy-start(f32[192,12,129]{2,0,1:T(8,128)S(1)} %fusion.7) | copy-start | bytes 3566596
  14.8 475.3 %copy-start.14 = (f32[192,12]{0,1:T(8,128)}, f32[192,12]{0,1:T(8,128)S(1)}, u32[]{:S(2)}) copy-start(f32[192,12]{0,1:T(8,128)S(1)} %slice_reduce_fusion) | copy-start | bytes 27652
  417.3 1.7 copy-start
  417.3 1.7 copy-start.6
  417.3 1.6 copy-start.7
  430.3 8.0 copy-start.16
  438.3 5.4 copy-start.17
  447.0 20.1 %all-to-all-start.5 = ((f32[16,1,144]{2,1,0:T(1,128)}), f32[16,1,144]{2,1,0:T(1,128)S(1)}, u32[]{:S(2)}, u32[]{:S(2)}) async-start(f32[16,1,144]{2,1,0:T(1,128)} %reshape.302), calls=%async_computation.5 | async-start | bytes 32768 | tf_op jit(solution)/shard_map/all_to_all | solution.py:140
  467.1 12.8 %all-to-all-start.4 = ((f32[16,1,144]{2,1,0:T(1,128)}), f32[16,1,144]{2,1,0:T(1,128)S(1)}, u32[]{:S(2)}, u32[]{:S(2)}) async-start(f32[16,1,144]{2,1,0:T(1,128)} %reshape.300), calls=%async_computation.4 | async-start | bytes 32768 | tf_op jit(solution)/shard_map/all_to_all | solution.py:137
  479.9 11.2 %all-to-all-start.8 = ((f32[16,1,144]{2,1,0:T(1,128)}), f32[16,1,144]{2,1,0:T(1,128)S(1)}, u32[]{:S(2)}, u32[]{:S(2)}) async-start(f32[16,1,144]{2,1,0:T(1,128)} %reshape.296), calls=%async_computation.8 | async-start | bytes 32768 | tf_op jit(solution)/shard_map/all_to_all | solution.py:140
  491.1 23.3 %copy-start.15 = (f32[192,12]{0,1:T(8,128)S(1)}, f32[192,12]{0,1:T(8,128)}, u32[]{:S(2)}) copy-start(f32[192,12]{0,1:T(8,128)} %copy-done.14) | copy-start | bytes 27652
  491.1 13.4 %all-to-all-start.7 = ((f32[16,1,144]{2,1,0:T(1,128)}), f32[16,1,144]{2,1,0:T(1,128)S(1)}, u32[]{:S(2)}, u32[]{:S(2)}) async-start(f32[16,1,144]{2,1,0:T(1,128)} %reshape.294), calls=%async_computation.7 | async-start | bytes 32768 | tf_op jit(solution)/shard_map/all_to_all | solution.py:137
  504.5 16.8 %all-to-all-start.6 = ((f32[16,1,144]{2,1,0:T(1,128)}), f32[16,1,144]{2,1,0:T(1,128)S(1)}, u32[]{:S(2)}, u32[]{:S(2)}) async-start(f32[16,1,144]{2,1,0:T(1,128)} %reshape.304), calls=%async_computation.6 | async-start | bytes 32768 | tf_op jit(solution)/shard_map/all_to_all | solution.py:147
  521.3 12.8 %all-to-all-start.9 = ((f32[16,1,144]{2,1,0:T(1,128)}), f32[16,1,144]{2,1,0:T(1,128)S(1)}, u32[]{:S(2)}, u32[]{:S(2)}) async-start(f32[16,1,144]{2,1,0:T(1,128)} %reshape.298), calls=%async_computation.9 | async-start | bytes 32768 | tf_op jit(solution)/shard_map/all_to_all | solution.py:147
  534.1 21.1 %copy-start.8 = (f32[16,1,144]{2,1,0:T(1,128)}, f32[16,1,144]{2,1,0:T(1,128)S(1)}, u32[]{:S(2)}) copy-start(f32[16,1,144]{2,1,0:T(1,128)S(1)} %all-to-all-done.9) | copy-start | bytes 27652
  534.1 11.0 %all-to-all-start.10 = ((f32[16,1,144]{2,1,0:T(1,128)}), f32[16,1,144]{2,1,0:T(1,128)S(1)}, u32[]{:S(2)}, u32[]{:S(2)}) async-start(f32[16,1,144]{2,1,0:T(1,128)} %reshape.308), calls=%async_computation.10 | async-start | bytes 32768 | tf_op jit(solution)/shard_map/all_to_all | solution.py:148
  545.2 10.1 %copy-start.10 = (f32[16,1,144]{2,1,0:T(1,128)}, f32[16,1,144]{2,1,0:T(1,128)S(1)}, u32[]{:S(2)}) copy-start(f32[16,1,144]{2,1,0:T(1,128)S(1)} %all-to-all-done.10) | copy-start | bytes 27652
  545.2 13.9 %all-to-all-start.11 = ((f32[16,1,144]{2,1,0:T(1,128)}), f32[16,1,144]{2,1,0:T(1,128)S(1)}, u32[]{:S(2)}, u32[]{:S(2)}) async-start(f32[16,1,144]{2,1,0:T(1,128)} %reshape.306), calls=%async_computation.11 | async-start | bytes 32768 | tf_op jit(solution)/shard_map/all_to_all | solution.py:148
  559.1 0.6 copy-start.12
  559.7 37.1 %all-to-all-start.2 = ((f32[1,12,192,256]{3,0,1,2:T(1,128)}), f32[1,12,192,256]{3,0,1,2:T(1,128)}, u32[]{:S(2)}, u32[]{:S(2)}) async-start(f32[1,12,192,256]{3,0,1,2:T(1,128)} %copy.86), calls=%async_computation.2 | async-start | bytes 4718592 | tf_op jit(solution)/shard_map/all_to_all | solution.py:136
  596.8 39.3 %all-to-all-start = ((f32[1,12,192,256]{3,0,1,2:T(1,128)}), f32[1,12,192,256]{3,0,1,2:T(1,128)}, u32[]{:S(2)}, u32[]{:S(2)}) async-start(f32[1,12,192,256]{3,0,1,2:T(1,128)} %copy.81), calls=%async_computation | async-start | bytes 4718592 | tf_op jit(solution)/shard_map/all_to_all | solution.py:136
  617.1 4.8 copy-start.2
  636.1 37.5 %all-to-all-start.3 = ((f32[1,192,12,256]{3,0,2,1:T(1,128)}), f32[1,192,12,256]{3,0,2,1:T(1,128)}, u32[]{:S(2)}, u32[]{:S(2)}) async-start(f32[1,192,12,256]{3,0,2,1:T(1,128)} %copy.89), calls=%async_computation.3 | async-start | bytes 4718592 | tf_op jit(solution)/shard_map/all_to_all | solution.py:146
  654.7 4.9 copy-start.3
  673.6 9.5 %copy-start.9 = (f32[16,1,144]{2,1,0:T(1,128)S(1)}, f32[16,1,144]{2,1,0:T(1,128)}, u32[]{:S(2)}) copy-start(f32[16,1,144]{2,1,0:T(1,128)} %copy-done.8) | copy-start | bytes 27652
  673.6 10.9 %copy-start.11 = (f32[16,1,144]{2,1,0:T(1,128)S(1)}, f32[16,1,144]{2,1,0:T(1,128)}, u32[]{:S(2)}) copy-start(f32[16,1,144]{2,1,0:T(1,128)} %copy-done.10) | copy-start | bytes 27652
  673.6 12.3 %copy-start.13 = (f32[16,1,144]{2,1,0:T(1,128)S(1)}, f32[16,1,144]{2,1,0:T(1,128)}, u32[]{:S(2)}) copy-start(f32[16,1,144]{2,1,0:T(1,128)} %copy-done.12) | copy-start | bytes 27652
  673.6 37.4 %all-to-all-start.1 = ((f32[1,192,12,256]{3,0,2,1:T(1,128)}), f32[1,192,12,256]{3,0,2,1:T(1,128)}, u32[]{:S(2)}, u32[]{:S(2)}) async-start(f32[1,192,12,256]{3,0,2,1:T(1,128)} %copy.84), calls=%async_computation.1 | async-start | bytes 4718592 | tf_op jit(solution)/shard_map/all_to_all | solution.py:146
  681.1 148.8 %reduce-scatter.2.cloned.1.call-start = ((), (), s32[]{:S(2)}) async-start(), calls=%async_computation.13 | async-start | bytes 3342336 | tf_op jit(solution)/shard_map/reduce_scatter | solution.py:161
  714.9 1.7 copy-start.5
  728.3 1.7 copy-start.1
Sparse Core Ops, SparseCore 0:
  10.4 395.9 all-gather.2
  739.8 90.0 reduce-scatter.1
